TPU v7x, 32 devices: a whole 2x2x4 slice. The times are simulated.
32 devices in a mesh: kt: 4 (over z), ks: 8 (over y, x, core).
Axes of the slice: x: 2, y: 2, z: 4, core: 2. Of those that a mesh axis runs over, the one named last changes fastest.
Arguments:
- val_target: bfloat16 [8, 32, 512], P('kt', None, 'ks'), may hold values from -6 to 6
- cond_target: bfloat16 [8, 64, 512], P('kt', None, 'ks'), may hold values from -0.046875 to 0.046875
- val_source: bfloat16 [32, 32, 512], P('ks', None, 'kt'), may hold values from -6 to 6
- cond_source: bfloat16 [32, 64, 512], P('ks', None, 'kt'), may hold values from -0.125 to 0.125
- trial_vectors: bfloat16 [32, 16, 2048], P('ks', 'kt'), may hold values from -6 to 6
- screened: bfloat16 [512, 512, 512], P(None, ('kt', 'ks')), may hold values from -0.25 to 0.25
- pair_momentum: int32 [8, 32], replicated, may hold values from 0 to 511
Outputs:
- kernel_out: float32 [8, 16, 2048], P('kt', 'ks')
All inputs are finite; a program needn't handle non-finite values.
Results may differ from a plain program's by a relative error of at most 0.019.
Values may be sent and summed in bfloat16 or wider, within the bound.
A program may use at most 128 MiB of HBM per device.

v0:
```python
import functools

import jax
import jax.numpy as jnp
from jax import lax
from jax.experimental import pallas as pl
from jax.experimental.pallas import tpu as pltpu
from jax.sharding import PartitionSpec as P


def general(val_target, cond_target, val_source, cond_source, trial_vectors, screened, pair_momentum):
    tgt_val, tgt_cond = (
        lax.all_gather(val_target, "ks", axis=2, tiled=True),
        lax.all_gather(cond_target, "ks", axis=2, tiled=True),
    )
    src_val, src_cond, vectors = (
        lax.all_gather(val_source, "kt", axis=2, tiled=True),
        lax.all_gather(cond_source, "kt", axis=2, tiled=True),
        lax.all_gather(trial_vectors, "kt", axis=1, tiled=True),
    )
    count_kt = lax.axis_size("kt")
    count_ks = lax.axis_size("ks")
    tgt_count = tgt_val.shape[0]
    src_count = src_val.shape[0]
    pair_count = tgt_count * src_count
    width = screened.shape[2]
    val_bands = tgt_val.shape[1]
    cond_bands = tgt_cond.shape[1]
    vec_count = vectors.shape[1]
    table = pair_momentum.reshape(count_kt, tgt_count, count_ks, src_count)
    table = table.transpose(1, 3, 0, 2).reshape(pair_count, count_kt * count_ks)
    outgoing = screened[table]
    arrived = lax.all_to_all(outgoing, ("kt", "ks"), split_axis=1, concat_axis=1, tiled=True)
    pair_mats = arrived.reshape(tgt_count, src_count, width, width)
    trial_four = vectors.reshape(src_count, vec_count, val_bands, cond_bands)
    dressed = jnp.einsum(
        "snwc,scq->snwq", trial_four, src_cond, preferred_element_type=jnp.float32
    ).astype(jnp.bfloat16)
    pair_prod = (
        tgt_val.astype(jnp.float32)[:, None, :, None, :]
        * src_val.astype(jnp.float32)[None, :, None, :, :]
    ).astype(jnp.bfloat16)
    kernels = jnp.einsum(
        "tsvwp,tspq->tsvwq", pair_prod, pair_mats, preferred_element_type=jnp.float32
    ).astype(jnp.bfloat16)
    reduced = jnp.einsum(
        "tsvwq,snwq->tvnq", kernels, dressed, preferred_element_type=jnp.float32
    ).astype(jnp.bfloat16)
    partial_out = jnp.einsum(
        "tvnq,tcq->tnvc", reduced, tgt_cond, preferred_element_type=jnp.float32
    )
    partial_out = partial_out.reshape(tgt_count, vec_count, val_bands * cond_bands)
    return lax.psum_scatter(
        partial_out.astype(jnp.bfloat16), "ks", scatter_dimension=1, tiled=True
    ).astype(jnp.float32)


MESH = pl.DeviceIdType.MESH
VMEM = pl.BlockSpec(memory_space=pltpu.VMEM)


def remote(src, dst, send, recv, kt, ks):
    return pltpu.make_async_remote_copy(
        src_ref=src, dst_ref=dst, send_sem=send, recv_sem=recv, device_id=(kt, ks), device_id_type=MESH
    )


def fused_kernel(nz, ns, nt, nsl, table, screened, block, vsx, vtx, result,
                 out, vsg, vtg, slab, wide, mbuf, abuf, sent, got,
                 zs, zr, xs, xr, ys, yr, as_, ar, bs, br, ps, pr, vss, vsr, vts, vtr, fs, fr, ls):
    z, k = lax.axis_index("kt"), lax.axis_index("ks")
    core = lax.rem(k, 2)
    side = lax.rem(k // 2, 2)
    kx = k + 2 - 4 * side
    ky = lax.rem(k + 4, ns)
    kd = lax.rem(kx + 4, ns)
    kp = k + 1 - 2 * core
    other = [kp, kx + 1 - 2 * core, lax.rem(kp + 4, ns), lax.rem(kx + 5 - 2 * core, ns)]
    half = block.shape[0] // 2
    first, second = pl.ds(0, half), pl.ds(half, half)
    zpeer = [lax.rem(z + j, nz) for j in range(nz)]
    speer = [lax.rem(k + j, ns) for j in range(ns)]
    me = z * ns + k
    count = nz * ns

    load = pltpu.make_async_copy(screened, slab, ls.at[3])
    load.start()
    own = [
        pltpu.make_async_copy(block, out.at[me], ls.at[0]),
        pltpu.make_async_copy(vsx.at[k], vsg.at[k], ls.at[1]),
        pltpu.make_async_copy(vtx, vtg.at[k], ls.at[2]),
    ]
    for copy in own:
        copy.start()

    barrier = pltpu.get_barrier_semaphore()

    def hello(j, carry):
        peer = lax.rem(me + j, count)
        pl.semaphore_signal(barrier, inc=1, device_id=(peer // ns, lax.rem(peer, ns)), device_id_type=MESH)
        return carry

    lax.fori_loop(1, count, hello, 0)
    pl.semaphore_wait(barrier, count - 1)

    slot = lambda zz, kk: out.at[zz * ns + kk]
    started = []

    def go(copy):
        copy.start()
        started.append(copy)

    def arrived(dst, recv):
        remote(dst, dst, recv, recv, z, kp).wait_recv()

    def partner(index, src, zz, kk):
        go(remote(src, slot(zz, kk), ps.at[index], pr.at[index], z, kp))

    for j in range(1, ns):
        go(remote(vsx.at[speer[j]], vsg.at[k], vss.at[j], vsr.at[j], z, speer[j]))
    for j in (1, nz - 1, *range(2, nz - 1)):
        go(remote(block, slot(z, k), zs.at[j], zr.at[nz - j], zpeer[j], k))
    go(remote(block, slot(z, k), xs.at[0], xr.at[0], z, kx))
    go(remote(block, slot(z, k), ys.at[0], yr.at[0], z, ky))
    partner(0, block, z, k)
    for j in range(1, ns):
        go(remote(vtx, vtg.at[k], vts.at[j], vtr.at[j], z, speer[j]))

    order = [0, 1, nz - 1, *range(2, nz - 1)]

    def spread(j):
        zz = zpeer[j]
        arrived(slot(zz, k), zr.at[j])
        go(remote(slot(zz, k), slot(zz, k), xs.at[j], xr.at[j], z, kx))
        go(remote(slot(zz, k), slot(zz, k), ys.at[j], yr.at[j], z, ky))
        partner(j, slot(zz, k), zz, k)

    def relay(j):
        zz = zpeer[j]
        arrived(slot(zz, kx), xr.at[j])
        go(remote(slot(zz, kx).at[first], slot(zz, kx).at[first], as_.at[j], ar.at[j], z, ky))
        partner(nz + j, slot(zz, kx), zz, kx)
        arrived(slot(zz, ky), yr.at[j])
        go(remote(slot(zz, ky).at[second], slot(zz, ky).at[second], bs.at[j], br.at[j], z, kx))
        partner(2 * nz + j, slot(zz, ky), zz, ky)

    def corner(j):
        zz = zpeer[j]
        arrived(slot(zz, kd).at[first], ar.at[j])
        arrived(slot(zz, kd).at[second], br.at[j])
        partner(3 * nz + j, slot(zz, kd), zz, kd)

    def passed(piece):
        for j in range(nz):
            arrived(slot(zpeer[j], other[piece]), pr.at[piece * nz + j])

    rows, width = slab.shape[1:]
    tgt = nz * nt
    nvec = mbuf.shape[1] // rows
    lanes = 128
    halves = nvec // nz // 2
    depth = vsg.shape[2] // nsl
    shape = (nsl * rows, nsl * depth)
    picked = lax.broadcasted_iota(jnp.int32, shape, 0) // rows == lax.broadcasted_iota(jnp.int32, shape, 1) // depth
    trial_rows = halves * nsl * depth
    cond = lanes // 2
    group = 4
    rblocks, qblocks = rows // 8, width // lanes

    def compute(b, fresh=False):
        low = lax.broadcasted_iota(jnp.int32, (rows, lanes), 1) < lanes // 2
        left = jnp.concatenate([vsg[b].astype(jnp.float32)] * nsl, axis=0)
        left = jnp.where(picked, left, 0.0).astype(jnp.bfloat16)
        right = jnp.concatenate(
            [out[zz * ns + b, h * nsl * depth:(h + 1) * nsl * depth, :] for zz in range(nz) for h in range(halves)],
            axis=1,
        )
        folded = jnp.dot(left, right, preferred_element_type=jnp.float32)
        for s in range(nsl):
            parts = []
            for j in range(nvec // 2):
                piece = folded[s * rows:(s + 1) * rows, j * lanes:(j + 1) * lanes]
                parts += [jnp.where(low, piece, 0.0), jnp.where(low, 0.0, piece)]
            left_s = jnp.concatenate(parts, axis=0).astype(jnp.bfloat16)
            at = trial_rows + s * cond
            cond_s = jnp.concatenate([out[zz * ns + b, at:at + cond, :] for zz in range(nz)], axis=1)
            right_s = jnp.concatenate([cond_s, cond_s], axis=0)
            mbuf[s] = jnp.dot(left_s, right_s, preferred_element_type=jnp.float32)

        def widen(t, carry):
            for s in range(nsl):
                wide[t * nsl + s] = slab[table[t, b * nsl + s]].astype(jnp.float32)
            return carry

        lax.fori_loop(0, tgt, widen, 0)

        def tile(i, carry):
            q = pl.ds(pl.multiple_of(lax.rem(i, qblocks) * lanes, lanes), lanes)
            rest = i // qblocks
            r = lax.rem(rest, rblocks) * 8
            n0 = (rest // rblocks) * group
            wrow = pl.ds(pl.multiple_of(r, 8), 8)
            mrow = [pl.ds(pl.multiple_of((n0 + g) * rows + r, 8), 8) for g in range(group)]
            total = {}
            for s in range(nsl):
                m = [mbuf[s, mrow[g], q] for g in range(group)]
                for t in range(tgt):
                    w = wide[t * nsl + s, wrow, q]
                    for g in range(group):
                        term = w * m[g]
                        total[t, g] = term if s == 0 else total[t, g] + term
            for t in range(tgt):
                for g in range(group):
                    value = total[t, g] if fresh else abuf[t, mrow[g], q] + total[t, g]
                    abuf[t, mrow[g], q] = value
            return carry

        lax.fori_loop(0, (nvec // group) * rblocks * qblocks, tile, 0)

    spread(order[1])
    relay(order[0])
    spread(order[2])
    relay(order[1])
    corner(order[0])
    for j in order[3:]:
        spread(j)
    for copy in own:
        copy.wait()
    for j in range(1, ns):
        arrived(vsg.at[speer[ns - j]], vsr.at[j])
    load.wait()
    compute(k, True)
    passed(0)
    compute(kp)
    relay(order[2])
    corner(order[1])
    for place in range(3, nz):
        relay(order[place])
    compute(kx)
    for place in range(2, nz - 1):
        corner(order[place])
    compute(ky)
    corner(order[-1])
    passed(1)
    passed(2)

    def later(i, carry):
        one = i // 2
        sx = lax.rem(i + 1, 2) * one + (1 - one) * lax.rem(i, 2)
        sy = (1 - one) + one * lax.rem(i, 2)
        kc = k + one * (1 - 2 * core)
        compute(lax.rem(kc + sx * (2 - 4 * side) + 4 * sy, ns))
        return carry

    lax.fori_loop(1, 4, later, 0)
    passed(3)
    compute(other[3])

    lowc = lax.broadcasted_iota(jnp.int32, (nvec * rows, lanes), 1) < lanes // 2
    at = trial_rows + nsl * cond
    chunk = sent.shape[1] // ns

    def deal(dz, dk):
        zz, kk = lax.rem(z + dz, nz), lax.rem(k + dk, ns)
        src = sent.at[zz, pl.ds(pl.multiple_of(kk * chunk, chunk), chunk)]
        return remote(src, got.at[me], fs.at[dz, dk], fr.at[dz, dk], zz, kk)

    def emit(i, carry):
        dz = lax.rem(i + 1, nz)
        zz = lax.rem(z + dz, nz)
        right = jnp.concatenate([out[zz * ns + b, at:, :] for b in range(ns)], axis=0)
        pair = [jnp.dot(abuf[zz * nt + t].astype(jnp.bfloat16), right, preferred_element_type=jnp.float32) for t in range(nt)]
        sent[zz] = jnp.where(lowc, pair[0], pair[1]).astype(jnp.bfloat16)

        def push(dk, carry):
            deal(dz, dk).start()
            return carry

        lax.fori_loop((i + 1) // nz, ns, push, 0)
        return carry

    lax.fori_loop(0, nz, emit, 0)
    mine = pltpu.make_async_copy(sent.at[z, pl.ds(pl.multiple_of(k * chunk, chunk), chunk)], got.at[me], ls.at[4])
    mine.start()
    mine.wait()
    for copy in started:
        copy.wait_send()
    for j in range(1, ns):
        arrived(vtg.at[speer[ns - j]], vtr.at[j])

    def settle(i, carry):
        dz, dk = i // ns, lax.rem(i, ns)
        deal(dz, dk).wait_send()
        giver = got.at[lax.rem(z + nz - dz, nz) * ns + lax.rem(k + ns - dk, ns)]
        remote(giver, giver, fs.at[dz, dk], fr.at[dz, dk], z, kp).wait_recv()
        return carry

    lax.fori_loop(1, count, settle, 0)
    left = jnp.concatenate([vtg[b] for b in range(ns)], axis=1)
    for n in range(result.shape[0]):
        right = jnp.concatenate([got[i, n * rows:(n + 1) * rows, :] for i in range(count)], axis=0)
        result[n] = jnp.dot(left, right, preferred_element_type=jnp.float32)


def local(val_target, cond_target, val_source, cond_source, trial_vectors, screened, pair_momentum):
    nz, ns = lax.axis_size("kt"), lax.axis_size("ks")
    nt, bands, pk = val_target.shape
    nc = cond_target.shape[1]
    nsl, _, pz = val_source.shape
    nv = trial_vectors.shape[1]
    rows, width = screened.shape[1:]
    nvec = nv * nz
    nloc = nvec // ns
    bf16, f32 = jnp.bfloat16, jnp.float32
    trial = trial_vectors.reshape(nsl, nv // 2, 2, bands, nc).transpose(1, 0, 3, 2, 4).reshape(-1, 2 * nc)
    block = jnp.concatenate(
        [trial, cond_source.reshape(nsl * nc, pz), cond_target.transpose(2, 0, 1).reshape(pk, nt * nc)], axis=0
    )
    vsx = val_source.reshape(nsl, bands, ns, rows).transpose(2, 3, 0, 1).reshape(ns, rows, nsl * bands)
    vtx = val_target.reshape(nt * bands, pk)
    dma = pltpu.SemaphoreType.DMA
    wide = pl.pallas_call(
        functools.partial(fused_kernel, nz, ns, nt, nsl),
        out_shape=jax.ShapeDtypeStruct((nloc, nt * bands, nt * nc), f32),
        in_specs=[pl.BlockSpec(memory_space=pltpu.SMEM), pl.BlockSpec(memory_space=pl.ANY)] + [VMEM] * 3,
        out_specs=VMEM,
        scratch_shapes=[
            pltpu.VMEM((nz * ns, *block.shape), bf16),
            pltpu.VMEM(vsx.shape, bf16),
            pltpu.VMEM((ns, *vtx.shape), bf16),
            pltpu.VMEM(screened.shape, bf16),
            pltpu.VMEM((nz * nt * nsl, rows, width), f32),
            pltpu.VMEM((nsl, nvec * rows, width), f32),
            pltpu.VMEM((nz * nt, nvec * rows, width), f32),
            pltpu.VMEM((nz, nvec * rows, nt * nc), bf16),
            pltpu.VMEM((nz * ns, nloc * rows, nt * nc), bf16),
        ]
        + [dma((nz,))] * 10 + [dma((4 * nz,))] * 2 + [dma((ns,))] * 4 + [dma((nz, ns))] * 2 + [dma((5,))],
        compiler_params=pltpu.CompilerParams(
            collective_id=0, has_side_effects=True, vmem_limit_bytes=48 * 2**20
        ),
        name="fused",
    )(pair_momentum, screened, block, vsx, vtx)
    wide = wide.reshape(nloc, nt, bands, nt, nc)
    result = jnp.stack([wide[:, t, :, t, :] for t in range(nt)], axis=0)
    return result.reshape(nt, nloc, bands * nc)


def fits(mesh, args):
    val_target, cond_target, val_source, cond_source, trial_vectors, screened, pair_momentum = args
    nz, ns = mesh.shape["kt"], mesh.shape["ks"]
    aux = val_target.shape[2]
    nt, nvec, nc = val_target.shape[0] // nz, trial_vectors.shape[1], cond_target.shape[1]
    rows = aux // (nz * ns)
    return (
        ns == 8 and nz >= 4 and nt == 2 and 2 * nc == 128 and aux // nz == 128 and rows == 16
        and nvec % (2 * nz) == 0 and nvec % ns == 0 and pair_momentum.size <= 256
    )


def solution(mesh):
    in_specs = (
        P("kt", None, "ks"),
        P("kt", None, "ks"),
        P("ks", None, "kt"),
        P("ks", None, "kt"),
        P("ks", "kt", None),
        P(None, ("kt", "ks"), None),
        P(),
    )
    out_specs = P("kt", "ks", None)

    def whole(*args):
        body = local if fits(mesh, args) else general
        return jax.shard_map(body, mesh=mesh, in_specs=in_specs, out_specs=out_specs, check_vma=False)(*args)

    return whole
```

profile of v0, /device:TPU:0, one launch (start us, length us, event | category | flops | bytes accessed | tf_op | source)
XLA Modules:
  0.0 70.7 jit_solution(10457076896071076660)
XLA Ops:
  0.0 0.8 %copy.15 = bf16[64,128]{1,0:T(8,128)(2,1)S(1)} copy(bf16[64,128]{0,1:T(8,128)(2,1)} %bitcast.15) | data formatting | bytes 32768 | tf_op jit(solution)/shard_map/reshape | solution.py:317
  0.8 0.9 %copy.13 = bf16[4,32,128]{1,2,0:T(8,128)(2,1)S(1)} copy(bf16[4,32,128]{2,1,0:T(8,128)(2,1)} %param.9) | data formatting | bytes 65536 | tf_op args[2]
  1.7 0.1 copy.14
  1.8 0.1 reshape.34.vsx
  2.0 1.0 %reshape.29 = bf16[4,2,2,32,64]{4,3,2,1,0:T(8,128)(2,1)S(1)} reshape(bf16[4,4,2048]{2,1,0:T(4,128)(2,1)} %param.11) | data formatting | bytes 131072 | tf_op jit(solution)/shard_map/reshape | solution.py:315
  3.0 0.1 copy.17
  3.1 0.1 reshape.30
  3.2 0.9 %pad_maximum_fusion.block = bf16[576,128]{1,0:T(8,128)(2,1)S(1)} fusion(bf16[64,128]{1,0:T(8,128)(2,1)S(1)} %copy.15, bf16[256,128]{1,0:T(8,128)(2,1)} %bitcast.14, bf16[256,128]{1,0:T(8,128)(2,1)S(1)} %reshape.30), kind=kLoop, calls=%fused_computation | loop fusion | flops 442368 | bytes 294912 | tf_op jit(solution)/shard_map/concatenate | solution.py:316
  4.1 0.0 copy-start
  4.1 0.7 %copy-done = bf16[2,32,64]{2,1,0:T(8,128)(2,1)S(1)} copy-done((bf16[2,32,64]{2,1,0:T(8,128)(2,1)S(1)}, bf16[2,32,64]{2,1,0:T(8,128)(2,1)}, u32[]{:S(2)}) %copy-start) | copy-done | bytes 8216
  4.8 0.0 copy-start.1
  4.8 0.7 copy-done.1
  5.5 64.1 %fused.1 = f32[2,64,128]{2,1,0:T(8,128)S(1)} custom-call(s32[8,32]{1,0:T(8,128)S(1)} %copy-done.1, bf16[512,16,512]{2,1,0:T(8,128)(2,1)} %screened.1, bf16[576,128]{1,0:T(8,128)(2,1)S(1)} %pad_maximum_fusion.block, bf16[8,16,128]{2,1,0:T(8,128)(2,1)S(1)} %reshape.34.vsx, bf16[64,64]{1,0:T(8,128)(2,1)S(1)} %bitcast.11), custom_call_target="tpu_custom_call" | custom-call | tf_op jit(solution)/shard_map/fused/pallas_call | solution.py:322
  69.5 0.1 reshape.36
  69.7 0.2 slice_reduce_fusion.1
  69.9 0.1 stack.7
  70.0 0.1 stack.8
  70.0 0.6 pad_maximum_fusion.1
Async XLA Ops:
  4.1 0.7 %copy-start = (bf16[2,32,64]{2,1,0:T(8,128)(2,1)S(1)}, bf16[2,32,64]{2,1,0:T(8,128)(2,1)}, u32[]{:S(2)}) copy-start(bf16[2,32,64]{2,1,0:T(8,128)(2,1)} %param.7) | copy-start | bytes 24580
  4.8 0.7 copy-start.1
where the time goes:
time: 71.1 us; the launch traced here: 70.7 us
  Pallas kernels  64.1 us (90%)
  local copies, waits for them, and re-layouts  5.05 us (7%)
  other arithmetic  1.48 us (2%)
    pallas_call x1, Pallas kernels, local(): pl.pallas_call(functools.partial(fused_kernel, nz, ns, nt, nsl), out_shap...  64.1 us
    unnamed x5, local copies, waits for them, and re-layouts  2.29 us

commit v1 on v0

--- a/solution.py
+++ b/solution.py
@@ -156,7 +156,7 @@
 
     rows, width = slab.shape[1:]
     tgt = nz * nt
-    nvec = mbuf.shape[1] // rows
+    nvec = mbuf.shape[2]
     lanes = 128
     halves = nvec // nz // 2
     depth = vsg.shape[2] // nsl
@@ -165,7 +165,7 @@
     trial_rows = halves * nsl * depth
     cond = lanes // 2
     group = 4
-    rblocks, qblocks = rows // 8, width // lanes
+    qblocks = width // lanes
 
     def compute(b, fresh=False):
         low = lax.broadcasted_iota(jnp.int32, (rows, lanes), 1) < lanes // 2
@@ -185,37 +185,33 @@
             at = trial_rows + s * cond
             cond_s = jnp.concatenate([out[zz * ns + b, at:at + cond, :] for zz in range(nz)], axis=1)
             right_s = jnp.concatenate([cond_s, cond_s], axis=0)
-            mbuf[s] = jnp.dot(left_s, right_s, preferred_element_type=jnp.float32)
+            full = jnp.dot(left_s, right_s, preferred_element_type=jnp.float32).astype(jnp.bfloat16)
+            for q in range(qblocks):
+                mbuf[q, s] = full[:, q * lanes:(q + 1) * lanes].reshape(nvec, rows, lanes)
 
         def widen(t, carry):
             for s in range(nsl):
-                wide[t * nsl + s] = slab[table[t, b * nsl + s]].astype(jnp.float32)
+                w = slab[table[t, b * nsl + s]]
+                for q in range(qblocks):
+                    wide[q, t * nsl + s] = w[:, q * lanes:(q + 1) * lanes]
             return carry
 
         lax.fori_loop(0, tgt, widen, 0)
 
-        def tile(i, carry):
-            q = pl.ds(pl.multiple_of(lax.rem(i, qblocks) * lanes, lanes), lanes)
-            rest = i // qblocks
-            r = lax.rem(rest, rblocks) * 8
-            n0 = (rest // rblocks) * group
-            wrow = pl.ds(pl.multiple_of(r, 8), 8)
-            mrow = [pl.ds(pl.multiple_of((n0 + g) * rows + r, 8), 8) for g in range(group)]
-            total = {}
-            for s in range(nsl):
-                m = [mbuf[s, mrow[g], q] for g in range(group)]
-                for t in range(tgt):
-                    w = wide[t * nsl + s, wrow, q]
-                    for g in range(group):
-                        term = w * m[g]
-                        total[t, g] = term if s == 0 else total[t, g] + term
-            for t in range(tgt):
-                for g in range(group):
-                    value = total[t, g] if fresh else abuf[t, mrow[g], q] + total[t, g]
-                    abuf[t, mrow[g], q] = value
+        def tile(q, carry):
+            for t0 in range(0, tgt, group):
+                w = [[wide[q, (t0 + t) * nsl + s] for s in range(nsl)] for t in range(group)]
+                for n in range(nvec):
+                    m = [mbuf[q, s, n] for s in range(nsl)]
+                    for t in range(group):
+                        terms = [w[t][s] * m[s] for s in range(nsl)]
+                        while len(terms) > 1:
+                            terms = [sum(terms[i:i + 2][1:], terms[i]) for i in range(0, len(terms), 2)]
+                        value = terms[0] if fresh else abuf[q, t0 + t, n] + terms[0]
+                        abuf[q, t0 + t, n] = value
             return carry
 
-        lax.fori_loop(0, (nvec // group) * rblocks * qblocks, tile, 0)
+        lax.fori_loop(0, qblocks, tile, 0)
 
     spread(order[1])
     relay(order[0])
@@ -269,7 +265,10 @@
         dz = lax.rem(i + 1, nz)
         zz = lax.rem(z + dz, nz)
         right = jnp.concatenate([out[zz * ns + b, at:, :] for b in range(ns)], axis=0)
-        pair = [jnp.dot(abuf[zz * nt + t].astype(jnp.bfloat16), right, preferred_element_type=jnp.float32) for t in range(nt)]
+        pair = []
+        for t in range(nt):
+            parts = [abuf[q, zz * nt + t].reshape(nvec * rows, lanes) for q in range(qblocks)]
+            pair.append(jnp.dot(jnp.concatenate(parts, axis=1), right, preferred_element_type=jnp.float32))
         sent[zz] = jnp.where(lowc, pair[0], pair[1]).astype(jnp.bfloat16)
 
         def push(dk, carry):
@@ -329,9 +328,9 @@
             pltpu.VMEM(vsx.shape, bf16),
             pltpu.VMEM((ns, *vtx.shape), bf16),
             pltpu.VMEM(screened.shape, bf16),
-            pltpu.VMEM((nz * nt * nsl, rows, width), f32),
-            pltpu.VMEM((nsl, nvec * rows, width), f32),
-            pltpu.VMEM((nz * nt, nvec * rows, width), f32),
+            pltpu.VMEM((width // 128, nz * nt * nsl, rows, 128), bf16),
+            pltpu.VMEM((width // 128, nsl, nvec, rows, 128), bf16),
+            pltpu.VMEM((width // 128, nz * nt, nvec, rows, 128), bf16),
             pltpu.VMEM((nz, nvec * rows, nt * nc), bf16),
             pltpu.VMEM((nz * ns, nloc * rows, nt * nc), bf16),
         ]

time: 71.1 us -> 57.5 us (0.81)
  Pallas kernels: 64.1 us -> 50.4 us
    pallas_call x1, Pallas kernels: 64.1 us -> 50.4 us  [local(): pl.pallas_call(functools.partial(fused_kernel, nz, ns, nt, nsl), out_shap...]
where the time goes in v1:
time: 57.5 us; the launch traced here: 57.1 us
  Pallas kernels  50.4 us (88%)
  local copies, waits for them, and re-layouts  5.05 us (9%)
  other arithmetic  1.48 us (3%)
    pallas_call x1, Pallas kernels, local(): pl.pallas_call(functools.partial(fused_kernel, nz, ns, nt, nsl), out_shap...  50.4 us
    unnamed x5, local copies, waits for them, and re-layouts  2.29 us
    reshape x3, local copies, waits for them, and re-layouts, local(): trial_vectors.reshape(nsl, nv // 2, 2, bands, nc).transpose(1, 0, 3, 2, 4)  1.22 us

profile of v1, /device:TPU:0, one launch (start us, length us, event | category | flops | bytes accessed | tf_op | source)
XLA Modules:
  0.0 57.1 jit_solution(9604639322600546519)
XLA Ops:
  0.0 0.8 %copy.15 = bf16[64,128]{1,0:T(8,128)(2,1)S(1)} copy(bf16[64,128]{0,1:T(8,128)(2,1)} %bitcast.15) | data formatting | bytes 32768 | tf_op jit(solution)/shard_map/reshape | solution.py:316
  0.8 0.9 %copy.13 = bf16[4,32,128]{1,2,0:T(8,128)(2,1)S(1)} copy(bf16[4,32,128]{2,1,0:T(8,128)(2,1)} %param.9) | data formatting | bytes 65536 | tf_op args[2]
  1.7 0.1 copy.14
  1.8 0.1 reshape.34.vsx
  2.0 1.0 %reshape.29 = bf16[4,2,2,32,64]{4,3,2,1,0:T(8,128)(2,1)S(1)} reshape(bf16[4,4,2048]{2,1,0:T(4,128)(2,1)} %param.11) | data formatting | bytes 131072 | tf_op jit(solution)/shard_map/reshape | solution.py:314
  3.0 0.1 copy.17
  3.1 0.1 reshape.30
  3.2 0.9 %pad_maximum_fusion.block = bf16[576,128]{1,0:T(8,128)(2,1)S(1)} fusion(bf16[64,128]{1,0:T(8,128)(2,1)S(1)} %copy.15, bf16[256,128]{1,0:T(8,128)(2,1)} %bitcast.14, bf16[256,128]{1,0:T(8,128)(2,1)S(1)} %reshape.30), kind=kLoop, calls=%fused_computation | loop fusion | flops 442368 | bytes 294912 | tf_op jit(solution)/shard_map/concatenate | solution.py:315
  4.1 0.0 copy-start
  4.1 0.7 %copy-done = bf16[2,32,64]{2,1,0:T(8,128)(2,1)S(1)} copy-done((bf16[2,32,64]{2,1,0:T(8,128)(2,1)S(1)}, bf16[2,32,64]{2,1,0:T(8,128)(2,1)}, u32[]{:S(2)}) %copy-start) | copy-done | bytes 8216
  4.8 0.0 copy-start.1
  4.8 0.7 %copy-done.1 = s32[8,32]{1,0:T(8,128)S(1)} copy-done((s32[8,32]{1,0:T(8,128)S(1)}, s32[8,32]{1,0:T(8,128)}, u32[]{:S(2)}) %copy-start.1) | copy-done | bytes 1048
  5.5 50.4 %fused.1 = f32[2,64,128]{2,1,0:T(8,128)S(1)} custom-call(s32[8,32]{1,0:T(8,128)S(1)} %copy-done.1, bf16[512,16,512]{2,1,0:T(8,128)(2,1)} %screened.1, bf16[576,128]{1,0:T(8,128)(2,1)S(1)} %pad_maximum_fusion.block, bf16[8,16,128]{2,1,0:T(8,128)(2,1)S(1)} %reshape.34.vsx, bf16[64,64]{1,0:T(8,128)(2,1)S(1)} %bitcast.11), custom_call_target="tpu_custom_call" | custom-call | tf_op jit(solution)/shard_map/fused/pallas_call | solution.py:321
  55.9 0.1 reshape.36
  56.1 0.2 slice_reduce_fusion.1
  56.3 0.1 stack.7
  56.3 0.1 stack.8
  56.4 0.6 %pad_maximum_fusion.1 = f32[2,2,2048]{2,1,0:T(2,128)} fusion(f32[1,2,2048]{2,1,0:T(2,128)S(1)} %stack.8, f32[1,2,2048]{2,1,0:T(2,128)S(1)} %stack.7), kind=kLoop, calls=%fused_computation.4 | loop fusion | flops 8192 | bytes 65536 | tf_op jit(solution)/shard_map/stack | solution.py:344
Async XLA Ops:
  4.1 0.7 %copy-start = (bf16[2,32,64]{2,1,0:T(8,128)(2,1)S(1)}, bf16[2,32,64]{2,1,0:T(8,128)(2,1)}, u32[]{:S(2)}) copy-start(bf16[2,32,64]{2,1,0:T(8,128)(2,1)} %param.7) | copy-start | bytes 24580
  4.8 0.7 %copy-start.1 = (s32[8,32]{1,0:T(8,128)S(1)}, s32[8,32]{1,0:T(8,128)}, u32[]{:S(2)}) copy-start(s32[8,32]{1,0:T(8,128)} %table.1) | copy-start | bytes 3076

commit v2 on v1

v2 whole, which is shorter than its diff:
```python
import functools

import jax
import jax.numpy as jnp
from jax import lax
from jax.experimental import pallas as pl
from jax.experimental.pallas import tpu as pltpu
from jax.sharding import PartitionSpec as P


def general(val_target, cond_target, val_source, cond_source, trial_vectors, screened, pair_momentum):
    tgt_val, tgt_cond = (
        lax.all_gather(val_target, "ks", axis=2, tiled=True),
        lax.all_gather(cond_target, "ks", axis=2, tiled=True),
    )
    src_val, src_cond, vectors = (
        lax.all_gather(val_source, "kt", axis=2, tiled=True),
        lax.all_gather(cond_source, "kt", axis=2, tiled=True),
        lax.all_gather(trial_vectors, "kt", axis=1, tiled=True),
    )
    count_kt = lax.axis_size("kt")
    count_ks = lax.axis_size("ks")
    tgt_count = tgt_val.shape[0]
    src_count = src_val.shape[0]
    pair_count = tgt_count * src_count
    width = screened.shape[2]
    val_bands = tgt_val.shape[1]
    cond_bands = tgt_cond.shape[1]
    vec_count = vectors.shape[1]
    table = pair_momentum.reshape(count_kt, tgt_count, count_ks, src_count)
    table = table.transpose(1, 3, 0, 2).reshape(pair_count, count_kt * count_ks)
    outgoing = screened[table]
    arrived = lax.all_to_all(outgoing, ("kt", "ks"), split_axis=1, concat_axis=1, tiled=True)
    pair_mats = arrived.reshape(tgt_count, src_count, width, width)
    trial_four = vectors.reshape(src_count, vec_count, val_bands, cond_bands)
    dressed = jnp.einsum(
        "snwc,scq->snwq", trial_four, src_cond, preferred_element_type=jnp.float32
    ).astype(jnp.bfloat16)
    pair_prod = (
        tgt_val.astype(jnp.float32)[:, None, :, None, :]
        * src_val.astype(jnp.float32)[None, :, None, :, :]
    ).astype(jnp.bfloat16)
    kernels = jnp.einsum(
        "tsvwp,tspq->tsvwq", pair_prod, pair_mats, preferred_element_type=jnp.float32
    ).astype(jnp.bfloat16)
    reduced = jnp.einsum(
        "tsvwq,snwq->tvnq", kernels, dressed, preferred_element_type=jnp.float32
    ).astype(jnp.bfloat16)
    partial_out = jnp.einsum(
        "tvnq,tcq->tnvc", reduced, tgt_cond, preferred_element_type=jnp.float32
    )
    partial_out = partial_out.reshape(tgt_count, vec_count, val_bands * cond_bands)
    return lax.psum_scatter(
        partial_out.astype(jnp.bfloat16), "ks", scatter_dimension=1, tiled=True
    ).astype(jnp.float32)


MESH = pl.DeviceIdType.MESH
HBM = pl.BlockSpec(memory_space=pltpu.MemorySpace.HBM)
C, X = range(2)
UP, DOWN, ACROSS_X, ACROSS_Y, HALF_Y, HALF_X, PARTNER = range(7)
LANES = 128


def remote(src, dst, send, recv, kt, ks):
    return pltpu.make_async_remote_copy(
        src_ref=src, dst_ref=dst, send_sem=send, recv_sem=recv, device_id=(kt, ks), device_id_type=MESH
    )


def nearest(nz):
    packed = []
    for place in range(nz):
        word = 0
        for own in range(nz):
            ranked = sorted(range(nz), key=lambda other: (abs(other - own), other))
            word |= ranked[place] << (2 * own)
        packed.append(word)
    return packed


def one_hot(shape, hit):
    row = lax.broadcasted_iota(jnp.int32, shape, 0)
    col = lax.broadcasted_iota(jnp.int32, shape, 1)
    return jnp.where(hit(row, col), 1.0, 0.0).astype(jnp.bfloat16)


def dot(a, b):
    return jnp.dot(a, b, preferred_element_type=jnp.float32)


def dot_t(a, b):
    return lax.dot_general(a, b, (((1,), (1,)), ((), ())), preferred_element_type=jnp.float32)


def fused_kernel(wbuf, mbuf, abuf, fbuf, nz, ns, table_in, screened, vt_in, ct_in, vs_in, cs_in, tr_in, result,
                 cb, xb, vsg, vtg, slab, trv, vsv, ctv, table, sent, got,
                 ss, rs, vss, vsr, vts, vtr, fs, fr, ls):
    bf16, f32 = jnp.bfloat16, jnp.float32
    z, k = lax.axis_index("kt"), lax.axis_index("ks")
    core, side, deep = lax.rem(k, 2), lax.rem(k // 2, 2), k // 4

    def flipped(c):
        return lax.rem(core + c % 2, 2) + 2 * lax.rem(side + (c // 2) % 2, 2) + 4 * lax.rem(deep + c // 4, 2)

    kk = [flipped(c) for c in range(ns)]
    kp, kx, ky, kd = kk[1], kk[2], kk[4], kk[6]
    me = z * ns + k
    z_up, z_down = z + 1, z - 1
    near = [lax.rem(lax.shift_right_logical(jnp.int32(word), 2 * z), 4) for word in nearest(nz)]
    bufs = [cb, xb]
    nsl, bands, depth = vs_in.shape
    nt, _, pk = vt_in.shape
    nc = ct_in.shape[1]
    nv = tr_in.shape[1]
    rows, width = slab.shape[1:]
    nsrc, tgt, nvec = ns * nsl, nz * nt, nz * nv
    half_w = bands // 2
    near_word = sum(near[j] * 4 ** j for j in range(nz))

    local = [
        (tr_in, trv), (vs_in, vsv), (ct_in, ctv), (cs_in, cb.at[me, pl.ds(0, nsl * nc)]), (vt_in, vtg.at[k]), (table_in, table), (screened, slab),
    ]
    local = [pltpu.make_async_copy(src, dst, ls.at[i]) for i, (src, dst) in enumerate(local)]
    for copy in local:
        copy.start()

    barrier = pltpu.get_barrier_semaphore()

    def greet(kt, ks):
        pl.semaphore_signal(barrier, inc=1, device_id=(kt, ks), device_id_type=MESH)

    has_up, has_down = z < nz - 1, z > 0
    for peer in (kp, kx, ky):
        greet(z, peer)
    pl.when(has_up)(lambda: greet(z + 1, k))
    pl.when(has_down)(lambda: greet(z - 1, k))

    local[2].wait()
    cb[me, nsl * nc:] = dot_t(one_hot((pk, pk), lambda r, c: r == c), ctv[...].reshape(nt * nc, pk)).astype(bf16)
    inner = jnp.logical_and(has_up, has_down)
    pl.when(inner)(lambda: pl.semaphore_wait(barrier, 5))
    pl.when(jnp.logical_not(inner))(lambda: pl.semaphore_wait(barrier, 4))

    started, guard = [], []

    def go(make, when=None):
        conds = guard + ([] if when is None else [when])
        started.append((make, conds))
        if when is None:
            make().start()
        else:
            pl.when(when)(lambda: make().start())

    def under(cond, body):
        guard.append(cond)
        pl.when(cond)(body)
        guard.pop()

    def both(d, body):
        if d == 0:
            body(z, None)
        else:
            for zz, there, below in ((z - d, z >= d, True), (z + d, z + d < nz, False)):
                under(there, functools.partial(body, zz, below))

    def slot(ty, zz, col):
        return bufs[ty].at[zz * ns + col]

    def part(ty, zz, col, second):
        n = bufs[ty].shape[1] // 2
        return slot(ty, zz, col).at[pl.ds(n * second, n)]

    def send(kind, ty, zz, col, kt, ks, when=None, src=None, second=None):
        def make():
            dst = slot(ty, zz, col) if second is None else part(ty, zz, col, second)
            return remote(dst if src is None else src, dst, ss.at[kind, ty, zz], rs.at[kind, ty, zz], kt, ks)

        go(make, when)

    def landed(kind, ty, zz, col, second=None):
        dst = slot(ty, zz, col) if second is None else part(ty, zz, col, second)
        remote(dst, dst, ss.at[kind, ty, zz], rs.at[kind, ty, zz], z, kp).wait_recv()

    def launch_z(ty, src=None):
        send(UP, ty, z, k, z_up, k, has_up, src)
        send(DOWN, ty, z, k, z_down, k, has_down, src)

    def launch_xy(ty):
        send(ACROSS_X, ty, z, k, z, kx)
        send(ACROSS_Y, ty, z, k, z, ky)
        send(PARTNER, ty, z, k, z, kp)

    def own(ty, d):
        def body(zz, below):
            landed(UP if below else DOWN, ty, zz, k)
            if below:
                send(UP, ty, zz, k, z_up, k, has_up)
            else:
                send(DOWN, ty, zz, k, z_down, k, has_down)
            send(ACROSS_X, ty, zz, k, z, kx)
            send(ACROSS_Y, ty, zz, k, z, ky)
            send(PARTNER, ty, zz, k, z, kp)

        both(d, body)

    def side_columns(ty, d):
        def body(zz, below):
            landed(ACROSS_X, ty, zz, kx)
            send(HALF_Y, ty, zz, kx, z, ky, second=0)
            landed(ACROSS_Y, ty, zz, ky)
            send(HALF_X, ty, zz, ky, z, kx, second=1)
            send(PARTNER + 1, ty, zz, kx, z, kp)
            send(PARTNER + 2, ty, zz, ky, z, kp)

        both(d, body)

    def diagonal(ty, d):
        def body(zz, below):
            landed(HALF_Y, ty, zz, kd, 0)
            landed(HALF_X, ty, zz, kd, 1)
            send(PARTNER + 3, ty, zz, kd, z, kp)

        both(d, body)

    def known(c):
        remote(vsg.at[0, kk[c]], vsg.at[0, kk[c]], vss.at[c], vsr.at[c], z, kp).wait_recv()

    def partner(ty, j, cols=range(4)):
        for i in cols:
            landed(PARTNER + i, ty, near[j], kk[2 * i + 1])

    def factors(c):
        go(lambda: remote(vsbuf.at[kk[c]], vsg.at[0, k], vss.at[c], vsr.at[c], z, kk[c]))
        go(lambda: remote(vt_in, vtg.at[k], vts.at[c], vtr.at[c], z, kk[c]))

    local[3].wait()
    launch_z(C)
    launch_xy(C)
    low = lax.broadcasted_iota(jnp.int32, (half_w, LANES), 1) < nc
    local[0].wait()
    order = one_hot((nv * half_w, nv * half_w), lambda r, c: c == lax.rem(r, half_w) * nv + r // half_w)
    for s in range(nsl):
        raw = trv[s].astype(f32)
        tall = jnp.concatenate([raw[:, i * LANES:(i + 1) * LANES] for i in range(half_w)], axis=0).astype(bf16)
        tall = dot(order, tall)
        for pair in range(nv // 2):
            even = tall[2 * pair * half_w:(2 * pair + 1) * half_w]
            odd = tall[(2 * pair + 1) * half_w:(2 * pair + 2) * half_w]
            first = jnp.where(low, even, pltpu.roll(odd, nc, 1))
            second = jnp.where(low, pltpu.roll(even, nc, 1), odd)
            at = (pair * nsl + s) * bands
            xb[me, at:at + bands, :] = jnp.concatenate([first, second], axis=0).astype(bf16)
    launch_z(X)
    launch_xy(X)
    local[1].wait()
    shuffle = one_hot(
        (nsl * bands, nsl * bands),
        lambda r, c: c == (r // bands) * bands + 2 * lax.rem(r, half_w) + lax.rem(r // half_w, 2),
    )
    eye = one_hot((depth, depth), lambda r, c: r == c)
    vsx = dot_t(eye, dot(shuffle, vsv[...].reshape(nsl * bands, depth)).astype(bf16)).astype(bf16)
    vsbuf = vsg.at[1]
    vsbuf[...] = vsx.reshape(ns, rows, nsl * bands)
    for c in (1, 2, 4):
        factors(c)
    keep = pltpu.make_async_copy(vsbuf.at[k], vsg.at[0, k], ls.at[7])
    keep.start()


    def widen(t, carry):
        for c in range(ns):
            for s in range(nsl):
                w = slab[table[t, kk[c] * nsl + s]]
                for q in range(nz):
                    wbuf[q, t, c * nsl + s] = w[:, q * LANES:(q + 1) * LANES]
        return carry

    picked = (
        lax.broadcasted_iota(jnp.int32, (nsl * rows, nsl * bands), 0) // rows
        == lax.broadcasted_iota(jnp.int32, (nsl * rows, nsl * bands), 1) // bands
    )

    def fold(places, cols):
        for zz, c in [(near[j], c) for j in places for c in cols]:
            left = jnp.concatenate([vsg[0, kk[c]].astype(f32)] * nsl, axis=0)
            left = jnp.where(picked, left, 0.0).astype(bf16)
            high = nsl * bands
            right = jnp.concatenate([xb[zz * ns + kk[c], i * high:(i + 1) * high] for i in range(nv // 2)], axis=1)
            folded = dot(left, right)
            for s in range(nsl):
                piece = []
                for n in range(nv):
                    wide = folded[s * rows:(s + 1) * rows, (n // 2) * LANES:(n // 2 + 1) * LANES]
                    wide = wide if n % 2 == 0 else pltpu.roll(wide, nc, 1)
                    piece.append(wide[:, :nc])
                fbuf[zz, c * nsl + s] = jnp.concatenate(piece, axis=0).astype(bf16)

    group_word = sum(g * 4 ** i for i, g in enumerate((0, 1, 0, 1, 2, 2, 3, 3)))
    pair_word = sum(p * 2 ** i for i, p in enumerate((0, 0, 1, 1, 0, 1, 0, 1)))

    def shifted(word, by, size):
        return lax.rem(lax.shift_right_logical(word, by), size)

    def unit(i, cols, add):
        g = shifted(near_word, 2 * shifted(jnp.int32(group_word), 2 * i, 4), 4)
        pair = shifted(jnp.int32(pair_word), i, 2)
        qs = [shifted(near_word, 4 * pair, 4), shifted(near_word, 4 * pair + 2, 4)]
        for c in cols:
            for s in range(nsl):
                right = jnp.concatenate([cb[q * ns + kk[c], s * nc:(s + 1) * nc] for q in qs], axis=1)
                full = dot(fbuf[g, c * nsl + s], right).astype(bf16)
                for h in range(2):
                    mbuf[h, c * nsl + s] = full[:, h * LANES:(h + 1) * LANES].reshape(nv, rows, LANES)
        for h, t0 in [(h, t0) for h in range(2) for t0 in range(0, tgt, 2)]:
            total = {}
            if add:
                total = {(t, n): abuf[t0 + t, g, qs[h], n] for t in range(2) for n in range(nv)}
            for c in cols:
                m = [[mbuf[h, c * nsl + s, n] for n in range(nv)] for s in range(nsl)]
                for t in range(2):
                    w = [wbuf[qs[h], t0 + t, c * nsl + s] for s in range(nsl)]
                    for n in range(nv):
                        four = (w[0] * m[0][n] + w[1] * m[1][n]) + (w[2] * m[2][n] + w[3] * m[3][n])
                        total[t, n] = total[t, n] + four if (t, n) in total else four
            for t in range(2):
                for n in range(nv):
                    abuf[t0 + t, g, qs[h], n] = total[t, n]

    NEAR, DIAG = (0, 1, 2, 3, 4, 5), (6, 7)

    def units(lo, hi, cols):
        def one(i, carry):
            unit(i, cols, cols is DIAG)
            return carry

        lax.fori_loop(lo, hi, one, 0)

    lowc = lax.broadcasted_iota(jnp.int32, (nv * rows, LANES), 1) < nc
    chunk = nv * rows // 2

    def deal(zz, col):
        src = sent.at[zz, col // 2, pl.ds(pl.multiple_of(lax.rem(col, 2) * chunk, chunk), chunk)]
        return remote(src, got.at[me], fs.at[zz, col], fr.at[z, k], zz, col)

    mine = pltpu.make_async_copy(
        sent.at[z, k // 2, pl.ds(pl.multiple_of(core * chunk, chunk), chunk)], got.at[me], ls.at[8]
    )

    def emit(j):
        g = near[j]

        for i in range(nz):
            zz = lax.rem(z + i + 1, nz)
            right = jnp.concatenate([cb[zz * ns + b, nsl * nc:] for b in range(ns)], axis=0)
            left = jnp.concatenate(
                [
                    jnp.concatenate([abuf[zz * nt + t, g, q].reshape(nv * rows, LANES) for q in range(nz)], axis=1)
                    for t in range(nt)
                ],
                axis=0,
            )
            full = dot(left, right)
            sent[zz, g] = jnp.where(lowc, full[:nv * rows], full[nv * rows:]).astype(bf16)
        for i in range(nz):
            zz = lax.rem(z + i + 1, nz)
            for h in range(2):
                if i < nz - 1:
                    deal(zz, 2 * g + h).start()
                else:
                    self = 2 * g + h == k
                    pl.when(jnp.logical_not(self))(lambda: deal(zz, 2 * g + h).start())
                    pl.when(self)(lambda: mine.start())

    own(C, 1)
    side_columns(C, 0)
    for c in (3, 5, 6):
        factors(c)
    own(X, 1)
    side_columns(X, 0)
    local[5].wait()
    local[6].wait()
    lax.fori_loop(0, tgt, widen, 0)
    own(C, 2)
    side_columns(C, 1)
    own(X, 2)
    side_columns(X, 1)
    own(C, 3)
    diagonal(C, 0)
    own(X, 3)
    known(6)
    factors(7)
    keep.wait()
    side_columns(C, 2)
    diagonal(X, 0)
    for c in range(1, 6):
        known(c)
    for j in (0, 1):
        partner(C, j, (0, 1, 2))
        partner(X, j, (0, 1, 2))
    fold((0, 1), NEAR)
    units(0, 2, NEAR)
    side_columns(C, 3)
    side_columns(X, 2)
    diagonal(C, 1)
    partner(C, 2, (0, 1, 2))
    partner(C, 3, (0, 1, 2))
    units(2, 4, NEAR)
    side_columns(X, 3)
    diagonal(X, 1)
    diagonal(C, 2)
    diagonal(C, 3)
    known(7)
    for j in (0, 1):
        partner(C, j, (3,))
        partner(X, j, (3,))
    fold((0, 1), DIAG)
    units(0, 2, DIAG)
    partner(X, 2, (0, 1, 2))
    partner(X, 3, (0, 1, 2))
    fold((2, 3), NEAR)
    units(4, 6, NEAR)
    diagonal(X, 2)
    diagonal(X, 3)
    partner(C, 2, (3,))
    partner(C, 3, (3,))
    units(2, 4, DIAG)
    emit(0)
    emit(1)
    units(6, 8, NEAR)
    partner(X, 2, (3,))
    partner(X, 3, (3,))
    fold((2, 3), DIAG)
    units(4, 6, DIAG)
    emit(2)
    units(6, 8, DIAG)
    emit(3)
    for make, conds in started:
        done = lambda make=make: make().wait_send()
        if conds:
            pl.when(functools.reduce(jnp.logical_and, conds))(done)
        else:
            done()
    local[4].wait()
    for c in range(1, ns):
        remote(vtg.at[kk[c]], vtg.at[kk[c]], vts.at[c], vtr.at[c], z, kp).wait_recv()
    parity = one_hot(
        (nt * bands, nt * bands),
        lambda r, c: c == lax.rem(r // half_w, nt) * bands + 2 * lax.rem(r, half_w) + r // (nt * half_w),
    )
    left = jnp.concatenate([vtg[b].reshape(nt * bands, pk) for b in range(ns)], axis=1)
    left = dot(parity, left).astype(bf16)
    mine.wait()

    def settle(i, carry):
        other = lax.rem(me + i, nz * ns)
        zz, col = other // ns, lax.rem(other, ns)
        deal(zz, col).wait_send()
        remote(got.at[other], got.at[other], fs.at[zz, col], fr.at[zz, col], z, kp).wait_recv()
        return carry

    lax.fori_loop(1, nz * ns, settle, 0)
    for n in range(result.shape[1]):
        right = jnp.concatenate([got[i, n * rows:(n + 1) * rows, :] for i in range(nz * ns)], axis=0)
        full = dot(left, right)
        for t in range(nt):
            even = full[t * half_w:(t + 1) * half_w]
            odd = full[(nt + t) * half_w:(nt + t + 1) * half_w]
            if t == 0:
                odd = pltpu.roll(odd, nc, 1)
            else:
                even = pltpu.roll(even, nc, 1)
            result[t, n] = jnp.where(low, even, odd)


def scoped(nz, ns, shapes, *refs):
    pl.run_scoped(
        lambda *bufs: fused_kernel(*bufs, nz, ns, *refs), *[pltpu.VMEM(shape, jnp.bfloat16) for shape in shapes]
    )


def local(val_target, cond_target, val_source, cond_source, trial_vectors, screened, pair_momentum):
    nz, ns = lax.axis_size("kt"), lax.axis_size("ks")
    nt, bands, pk = val_target.shape
    nc = cond_target.shape[1]
    nsl, _, pz = val_source.shape
    nv = trial_vectors.shape[1]
    rows, width = screened.shape[1:]
    nvec = nv * nz
    nloc = nvec // ns
    bf16, f32 = jnp.bfloat16, jnp.float32
    count, nsrc = nz * ns, ns * nsl
    shapes = [
        (nz, nz * nt, nsrc, rows, LANES),
        (2, nsrc, nv, rows, LANES),
        (nz * nt, nz, nz, nv, rows, LANES),
        (nz, nsrc, nv * rows, nc),
    ]
    dma = pltpu.SemaphoreType.DMA
    out = pl.pallas_call(
        functools.partial(scoped, nz, ns, shapes),
        out_shape=jax.ShapeDtypeStruct((nt, nloc, bands // 2, LANES), f32),
        in_specs=[HBM] * 7,
        out_specs=pl.BlockSpec(memory_space=pltpu.VMEM),
        scratch_shapes=[
            pltpu.VMEM((count, nsl * nc + pk, LANES), bf16),
            pltpu.VMEM((count, nv // 2 * nsl * bands, LANES), bf16),
            pltpu.VMEM((2, ns, rows, nsl * bands), bf16),
            pltpu.VMEM((ns, *val_target.shape), bf16),
            pltpu.VMEM(screened.shape, bf16),
            pltpu.VMEM(trial_vectors.shape, bf16),
            pltpu.VMEM(val_source.shape, bf16),
            pltpu.VMEM(cond_target.shape, bf16),
            pltpu.SMEM(pair_momentum.shape, jnp.int32),
            pltpu.VMEM((nz, nz, nv * rows, nt * nc), bf16),
            pltpu.VMEM((count, nloc * rows, nt * nc), bf16),
            dma((PARTNER + 4, 2, nz)), dma((PARTNER + 4, 2, nz)),
            dma((ns,)), dma((ns,)), dma((ns,)), dma((ns,)), dma((nz, ns)), dma((nz, ns)), dma((9,)),
        ],
        compiler_params=pltpu.CompilerParams(
            collective_id=0, has_side_effects=True, vmem_limit_bytes=67_043_328
        ),
        name="fused",
    )(pair_momentum, screened, val_target, cond_target, val_source, cond_source.reshape(nsl * nc, pz), trial_vectors)
    return out.reshape(nt, nloc, bands * nc)


def fits(mesh, args):
    val_target, cond_target, val_source, cond_source, trial_vectors, screened, pair_momentum = args
    nz, ns = mesh.shape["kt"], mesh.shape["ks"]
    aux = val_target.shape[2]
    nt, nvec, nc = val_target.shape[0] // nz, trial_vectors.shape[1], cond_target.shape[1]
    rows, bands = aux // (nz * ns), val_target.shape[1]
    nsl = val_source.shape[0] // ns
    return (
        ns == 8 and nz == 4 and nt == 2 and 2 * nc == LANES and aux // nz == LANES and rows == 16 and nsl == 4
        and bands == 32 and nvec == 4 * nz and nvec % ns == 0
    )


def solution(mesh):
    in_specs = (
        P("kt", None, "ks"),
        P("kt", None, "ks"),
        P("ks", None, "kt"),
        P("ks", None, "kt"),
        P("ks", "kt", None),
        P(None, ("kt", "ks"), None),
        P(),
    )
    out_specs = P("kt", "ks", None)

    def whole(*args):
        body = local if fits(mesh, args) else general
        return jax.shard_map(body, mesh=mesh, in_specs=in_specs, out_specs=out_specs, check_vma=False)(*args)

    return whole
```

time: 57.5 us -> 44.2 us (0.77)
  Pallas kernels: 50.4 us -> 42.6 us
  local copies, waits for them, and re-layouts: 5.05 us -> 1.39 us
  other arithmetic: 1.48 us -> 0 us
    pallas_call x1, Pallas kernels: 50.4 us -> 42.6 us  [local(): pl.pallas_call(functools.partial(scoped, nz, ns, shapes), out_shape=jax.S...]
    unnamed x5 -> x0, local copies, waits for them, and re-layouts: 2.29 us -> none
    reshape x6 -> x1, local copies, waits for them, and re-layouts: 2.3 us -> 1.39 us  [local(): return out.reshape(nt, nloc, bands * nc)]
    concatenate x1 -> x0, other arithmetic: 0.85 us -> none  [local(): jnp.concatenate([trial, cond_source.reshape(nsl * nc, pz), cond_target.tr...]
    another operation x1 -> x0, other arithmetic: 0.63 us -> none  [local(): result = jnp.stack([wide[:, t, :, t, :] for t in range(nt)], axis=0)]
where the time goes in v2:
time: 44.2 us; the launch traced here: 44 us
  Pallas kernels  42.6 us (96%)
  local copies, waits for them, and re-layouts  1.39 us (3%)
    pallas_call x1, Pallas kernels, local(): pl.pallas_call(functools.partial(scoped, nz, ns, shapes), out_shape=jax.S...  42.6 us
    reshape x1, local copies, waits for them, and re-layouts, local(): return out.reshape(nt, nloc, bands * nc)  1.39 us

profile of v2, /device:TPU:0, one launch (start us, length us, event | category | flops | bytes accessed | tf_op | source)
XLA Modules:
  0.0 44.0 jit_solution(17220150912383613312)
XLA Ops:
  0.0 42.6 %fused.1 = f32[2,2,16,128]{3,2,1,0:T(8,128)} custom-call(s32[8,32]{1,0:T(8,128)} %refs_0_.1, bf16[512,16,512]{2,1,0:T(8,128)(2,1)} %refs_1_.1, bf16[2,32,64]{2,1,0:T(8,128)(2,1)} %refs_2_.1, bf16[2,64,64]{2,1,0:T(8,128)(2,1)} %refs_3_.1, bf16[4,32,128]{2,1,0:T(8,128)(2,1)} %refs_4_.1, bf16[256,128]{1,0:T(8,128)(2,1)} %bitcast.3, bf16[4,4,2048]{2,1,0:T(4,128)(2,1)} %refs_6_.1), custom_call_target="tpu_custom_call" | custom-call | tf_op jit(solution)/shard_map/fused/pallas_call | solution.py:500
  42.6 1.4 %reshape.7 = f32[2,2,2048]{2,1,0:T(2,128)} reshape(f32[2,2,16,128]{3,2,1,0:T(8,128)} %fused.1) | data formatting | bytes 65536 | tf_op jit(solution)/shard_map/reshape | solution.py:525

commit v3 on v2

--- a/solution.py
+++ b/solution.py
@@ -58,7 +58,7 @@
 MESH = pl.DeviceIdType.MESH
 HBM = pl.BlockSpec(memory_space=pltpu.MemorySpace.HBM)
 C, X = range(2)
-UP, DOWN, ACROSS_X, ACROSS_Y, HALF_Y, HALF_X, PARTNER = range(7)
+UP, DOWN, ACROSS_X, ACROSS_Y, HALF_Y, HALF_X, DIAG_UP, DIAG_DOWN, PARTNER = range(9)
 LANES = 128
 
 
@@ -93,7 +93,7 @@
     return lax.dot_general(a, b, (((1,), (1,)), ((), ())), preferred_element_type=jnp.float32)
 
 
-def fused_kernel(wbuf, mbuf, abuf, fbuf, nz, ns, table_in, screened, vt_in, ct_in, vs_in, cs_in, tr_in, result,
+def fused_kernel(wbuf, mbuf, nbuf, abuf, fbuf, nz, ns, table_in, screened, vt_in, ct_in, vs_in, cs_in, tr_in, result,
                  cb, xb, vsg, vtg, slab, trv, vsv, ctv, table, sent, got,
                  ss, rs, vss, vsr, vts, vtr, fs, fr, ls):
     bf16, f32 = jnp.bfloat16, jnp.float32
@@ -119,7 +119,7 @@
     near_word = sum(near[j] * 4 ** j for j in range(nz))
 
     local = [
-        (tr_in, trv), (vs_in, vsv), (ct_in, ctv), (cs_in, cb.at[me, pl.ds(0, nsl * nc)]), (vt_in, vtg.at[k]), (table_in, table), (screened, slab),
+        (tr_in, trv), (vs_in, vsv), (ct_in, ctv), (cs_in, cb.at[me]), (vt_in, vtg.at[k]), (table_in, table), (screened, slab),
     ]
     local = [pltpu.make_async_copy(src, dst, ls.at[i]) for i, (src, dst) in enumerate(local)]
     for copy in local:
@@ -136,8 +136,6 @@
     pl.when(has_up)(lambda: greet(z + 1, k))
     pl.when(has_down)(lambda: greet(z - 1, k))
 
-    local[2].wait()
-    cb[me, nsl * nc:] = dot_t(one_hot((pk, pk), lambda r, c: r == c), ctv[...].reshape(nt * nc, pk)).astype(bf16)
     inner = jnp.logical_and(has_up, has_down)
     pl.when(inner)(lambda: pl.semaphore_wait(barrier, 5))
     pl.when(jnp.logical_not(inner))(lambda: pl.semaphore_wait(barrier, 4))
@@ -207,9 +205,11 @@
     def side_columns(ty, d):
         def body(zz, below):
             landed(ACROSS_X, ty, zz, kx)
-            send(HALF_Y, ty, zz, kx, z, ky, second=0)
+            if d != 1:
+                send(HALF_Y, ty, zz, kx, z, ky, second=0)
             landed(ACROSS_Y, ty, zz, ky)
-            send(HALF_X, ty, zz, ky, z, kx, second=1)
+            if d != 1:
+                send(HALF_X, ty, zz, ky, z, kx, second=1)
             send(PARTNER + 1, ty, zz, kx, z, kp)
             send(PARTNER + 2, ty, zz, ky, z, kp)
 
@@ -217,8 +217,14 @@
 
     def diagonal(ty, d):
         def body(zz, below):
-            landed(HALF_Y, ty, zz, kd, 0)
-            landed(HALF_X, ty, zz, kd, 1)
+            if d == 1:
+                landed(DIAG_UP if below else DIAG_DOWN, ty, zz, kd)
+            else:
+                landed(HALF_Y, ty, zz, kd, 0)
+                landed(HALF_X, ty, zz, kd, 1)
+            if d == 0:
+                send(DIAG_UP, ty, zz, kd, z_up, k, has_up)
+                send(DIAG_DOWN, ty, zz, kd, z_down, k, has_down)
             send(PARTNER + 3, ty, zz, kd, z, kp)
 
         both(d, body)
@@ -251,6 +257,8 @@
             second = jnp.where(low, pltpu.roll(even, nc, 1), odd)
             at = (pair * nsl + s) * bands
             xb[me, at:at + bands, :] = jnp.concatenate([first, second], axis=0).astype(bf16)
+    local[2].wait()
+    xb[me, nv // 2 * nsl * bands:] = dot_t(one_hot((pk, pk), lambda r, c: r == c), ctv[...].reshape(nt * nc, pk)).astype(bf16)
     launch_z(X)
     launch_xy(X)
     local[1].wait()
@@ -302,22 +310,28 @@
     def shifted(word, by, size):
         return lax.rem(lax.shift_right_logical(word, by), size)
 
-    def unit(i, cols, add):
+    def place(i):
         g = shifted(near_word, 2 * shifted(jnp.int32(group_word), 2 * i, 4), 4)
         pair = shifted(jnp.int32(pair_word), i, 2)
-        qs = [shifted(near_word, 4 * pair, 4), shifted(near_word, 4 * pair + 2, 4)]
+        return g, [shifted(near_word, 4 * pair, 4), shifted(near_word, 4 * pair + 2, 4)]
+
+    def expand(buf, i, cols):
+        g, qs = place(i)
         for c in cols:
             for s in range(nsl):
                 right = jnp.concatenate([cb[q * ns + kk[c], s * nc:(s + 1) * nc] for q in qs], axis=1)
                 full = dot(fbuf[g, c * nsl + s], right).astype(bf16)
                 for h in range(2):
-                    mbuf[h, c * nsl + s] = full[:, h * LANES:(h + 1) * LANES].reshape(nv, rows, LANES)
+                    buf[h, c * nsl + s] = full[:, h * LANES:(h + 1) * LANES].reshape(nv, rows, LANES)
+
+    def contract(buf, i, cols, add):
+        g, qs = place(i)
         for h, t0 in [(h, t0) for h in range(2) for t0 in range(0, tgt, 2)]:
             total = {}
             if add:
                 total = {(t, n): abuf[t0 + t, g, qs[h], n] for t in range(2) for n in range(nv)}
             for c in cols:
-                m = [[mbuf[h, c * nsl + s, n] for n in range(nv)] for s in range(nsl)]
+                m = [[buf[h, c * nsl + s, n] for n in range(nv)] for s in range(nsl)]
                 for t in range(2):
                     w = [wbuf[qs[h], t0 + t, c * nsl + s] for s in range(nsl)]
                     for n in range(nv):
@@ -330,11 +344,11 @@
     NEAR, DIAG = (0, 1, 2, 3, 4, 5), (6, 7)
 
     def units(lo, hi, cols):
-        def one(i, carry):
-            unit(i, cols, cols is DIAG)
-            return carry
-
-        lax.fori_loop(lo, hi, one, 0)
+        turns = [(buf, i) for buf, i in zip((mbuf, nbuf), range(lo, hi))]
+        for buf, i in turns:
+            expand(buf, i, cols)
+        for buf, i in turns:
+            contract(buf, i, cols, cols is DIAG)
 
     lowc = lax.broadcasted_iota(jnp.int32, (nv * rows, LANES), 1) < nc
     chunk = nv * rows // 2
@@ -352,7 +366,7 @@
 
         for i in range(nz):
             zz = lax.rem(z + i + 1, nz)
-            right = jnp.concatenate([cb[zz * ns + b, nsl * nc:] for b in range(ns)], axis=0)
+            right = jnp.concatenate([xb[zz * ns + b, nv // 2 * nsl * bands:] for b in range(ns)], axis=0)
             left = jnp.concatenate(
                 [
                     jnp.concatenate([abuf[zz * nt + t, g, q].reshape(nv * rows, LANES) for q in range(nz)], axis=1)
@@ -383,16 +397,13 @@
     lax.fori_loop(0, tgt, widen, 0)
     own(C, 2)
     side_columns(C, 1)
+    diagonal(C, 0)
     own(X, 2)
+    own(C, 3)
     side_columns(X, 1)
-    own(C, 3)
-    diagonal(C, 0)
-    own(X, 3)
     known(6)
     factors(7)
     keep.wait()
-    side_columns(C, 2)
-    diagonal(X, 0)
     for c in range(1, 6):
         known(c)
     for j in (0, 1):
@@ -400,9 +411,12 @@
         partner(X, j, (0, 1, 2))
     fold((0, 1), NEAR)
     units(0, 2, NEAR)
+    diagonal(X, 0)
+    own(X, 3)
+    side_columns(C, 2)
+    diagonal(C, 1)
     side_columns(C, 3)
     side_columns(X, 2)
-    diagonal(C, 1)
     partner(C, 2, (0, 1, 2))
     partner(C, 3, (0, 1, 2))
     units(2, 4, NEAR)
@@ -410,26 +424,26 @@
     diagonal(X, 1)
     diagonal(C, 2)
     diagonal(C, 3)
+    partner(X, 2, (0, 1, 2))
+    partner(X, 3, (0, 1, 2))
+    fold((2, 3), NEAR)
+    units(4, 6, NEAR)
+    diagonal(X, 2)
+    diagonal(X, 3)
     known(7)
     for j in (0, 1):
         partner(C, j, (3,))
         partner(X, j, (3,))
     fold((0, 1), DIAG)
     units(0, 2, DIAG)
-    partner(X, 2, (0, 1, 2))
-    partner(X, 3, (0, 1, 2))
-    fold((2, 3), NEAR)
-    units(4, 6, NEAR)
-    diagonal(X, 2)
-    diagonal(X, 3)
     partner(C, 2, (3,))
     partner(C, 3, (3,))
     units(2, 4, DIAG)
-    emit(0)
-    emit(1)
     units(6, 8, NEAR)
     partner(X, 2, (3,))
     partner(X, 3, (3,))
+    emit(0)
+    emit(1)
     fold((2, 3), DIAG)
     units(4, 6, DIAG)
     emit(2)
@@ -493,6 +507,7 @@
     shapes = [
         (nz, nz * nt, nsrc, rows, LANES),
         (2, nsrc, nv, rows, LANES),
+        (2, nsrc, nv, rows, LANES),
         (nz * nt, nz, nz, nv, rows, LANES),
         (nz, nsrc, nv * rows, nc),
     ]
@@ -503,8 +518,8 @@
         in_specs=[HBM] * 7,
         out_specs=pl.BlockSpec(memory_space=pltpu.VMEM),
         scratch_shapes=[
-            pltpu.VMEM((count, nsl * nc + pk, LANES), bf16),
-            pltpu.VMEM((count, nv // 2 * nsl * bands, LANES), bf16),
+            pltpu.VMEM((count, nsl * nc, LANES), bf16),
+            pltpu.VMEM((count, nv // 2 * nsl * bands + pk, LANES), bf16),
             pltpu.VMEM((2, ns, rows, nsl * bands), bf16),
             pltpu.VMEM((ns, *val_target.shape), bf16),
             pltpu.VMEM(screened.shape, bf16),

time: 44.2 us -> 42.3 us (0.957)
  Pallas kernels: 42.6 us -> 40.7 us
    pallas_call x1, Pallas kernels: 42.6 us -> 40.7 us  [local(): pl.pallas_call(functools.partial(scoped, nz, ns, shapes), out_shape=jax.S...]
where the time goes in v3:
time: 42.3 us; the launch traced here: 42.1 us
  Pallas kernels  40.7 us (96%)
  local copies, waits for them, and re-layouts  1.39 us (3%)
    pallas_call x1, Pallas kernels, local(): pl.pallas_call(functools.partial(scoped, nz, ns, shapes), out_shape=jax.S...  40.7 us
    reshape x1, local copies, waits for them, and re-layouts, local(): return out.reshape(nt, nloc, bands * nc)  1.39 us

profile of v3, /device:TPU:0, one launch (start us, length us, event | category | flops | bytes accessed | tf_op | source)
XLA Modules:
  0.0 42.1 jit_solution(4446752490479389331)
XLA Ops:
  0.0 40.7 %fused.1 = f32[2,2,16,128]{3,2,1,0:T(8,128)} custom-call(s32[8,32]{1,0:T(8,128)} %refs_0_.1, bf16[512,16,512]{2,1,0:T(8,128)(2,1)} %refs_1_.1, bf16[2,32,64]{2,1,0:T(8,128)(2,1)} %refs_2_.1, bf16[2,64,64]{2,1,0:T(8,128)(2,1)} %refs_3_.1, bf16[4,32,128]{2,1,0:T(8,128)(2,1)} %refs_4_.1, bf16[256,128]{1,0:T(8,128)(2,1)} %bitcast.3, bf16[4,4,2048]{2,1,0:T(4,128)(2,1)} %refs_6_.1), custom_call_target="tpu_custom_call" | custom-call | tf_op jit(solution)/shard_map/fused/pallas_call | solution.py:515
  40.8 1.4 %reshape.7 = f32[2,2,2048]{2,1,0:T(2,128)} reshape(f32[2,2,16,128]{3,2,1,0:T(8,128)} %fused.1) | data formatting | bytes 65536 | tf_op jit(solution)/shard_map/reshape | solution.py:540

commit v4 on v3

--- a/solution.py
+++ b/solution.py
@@ -341,14 +341,14 @@
                 for n in range(nv):
                     abuf[t0 + t, g, qs[h], n] = total[t, n]
 
-    NEAR, DIAG = (0, 1, 2, 3, 4, 5), (6, 7)
+    OWN, SIDE, NEAR, DIAG = (0, 1), (2, 3, 4, 5), (0, 1, 2, 3, 4, 5), (6, 7)
 
     def units(lo, hi, cols):
         turns = [(buf, i) for buf, i in zip((mbuf, nbuf), range(lo, hi))]
         for buf, i in turns:
             expand(buf, i, cols)
         for buf, i in turns:
-            contract(buf, i, cols, cols is DIAG)
+            contract(buf, i, cols, cols in (SIDE, DIAG))
 
     lowc = lax.broadcasted_iota(jnp.int32, (nv * rows, LANES), 1) < nc
     chunk = nv * rows // 2
@@ -376,7 +376,7 @@
             )
             full = dot(left, right)
             sent[zz, g] = jnp.where(lowc, full[:nv * rows], full[nv * rows:]).astype(bf16)
-        for i in range(nz):
+        for i in (nz // 2 - 1, *range(nz // 2 - 1), *range(nz // 2, nz)):
             zz = lax.rem(z + i + 1, nz)
             for h in range(2):
                 if i < nz - 1:
@@ -386,15 +386,15 @@
                     pl.when(jnp.logical_not(self))(lambda: deal(zz, 2 * g + h).start())
                     pl.when(self)(lambda: mine.start())
 
+    local[5].wait()
+    local[6].wait()
+    lax.fori_loop(0, tgt, widen, 0)
     own(C, 1)
     side_columns(C, 0)
     for c in (3, 5, 6):
         factors(c)
     own(X, 1)
     side_columns(X, 0)
-    local[5].wait()
-    local[6].wait()
-    lax.fori_loop(0, tgt, widen, 0)
     own(C, 2)
     side_columns(C, 1)
     diagonal(C, 0)
@@ -420,14 +420,18 @@
     partner(C, 2, (0, 1, 2))
     partner(C, 3, (0, 1, 2))
     units(2, 4, NEAR)
+    for j in (2, 3):
+        partner(X, j, (0,))
+    fold((2, 3), OWN)
+    units(4, 6, OWN)
     side_columns(X, 3)
     diagonal(X, 1)
     diagonal(C, 2)
     diagonal(C, 3)
-    partner(X, 2, (0, 1, 2))
-    partner(X, 3, (0, 1, 2))
-    fold((2, 3), NEAR)
-    units(4, 6, NEAR)
+    partner(X, 2, (1, 2))
+    partner(X, 3, (1, 2))
+    fold((2, 3), SIDE)
+    units(4, 6, SIDE)
     diagonal(X, 2)
     diagonal(X, 3)
     known(7)

time: 42.3 us -> 42.2 us (level)
  no operation moved by 1% of the time
where the time goes in v4:
time: 42.2 us; the launch traced here: 42 us
  Pallas kernels  40.6 us (96%)
  local copies, waits for them, and re-layouts  1.39 us (3%)
    pallas_call x1, Pallas kernels, local(): pl.pallas_call(functools.partial(scoped, nz, ns, shapes), out_shape=jax.S...  40.6 us
    reshape x1, local copies, waits for them, and re-layouts, local(): return out.reshape(nt, nloc, bands * nc)  1.39 us

profile of v4, /device:TPU:0, one launch (start us, length us, event | category | flops | bytes accessed | tf_op | source)
XLA Modules:
  0.0 42.0 jit_solution(1320955244901456872)
XLA Ops:
  0.0 40.6 %fused.1 = f32[2,2,16,128]{3,2,1,0:T(8,128)} custom-call(s32[8,32]{1,0:T(8,128)} %refs_0_.1, bf16[512,16,512]{2,1,0:T(8,128)(2,1)} %refs_1_.1, bf16[2,32,64]{2,1,0:T(8,128)(2,1)} %refs_2_.1, bf16[2,64,64]{2,1,0:T(8,128)(2,1)} %refs_3_.1, bf16[4,32,128]{2,1,0:T(8,128)(2,1)} %refs_4_.1, bf16[256,128]{1,0:T(8,128)(2,1)} %bitcast.3, bf16[4,4,2048]{2,1,0:T(4,128)(2,1)} %refs_6_.1), custom_call_target="tpu_custom_call" | custom-call | tf_op jit(solution)/shard_map/fused/pallas_call | solution.py:519
  40.6 1.4 %reshape.7 = f32[2,2,2048]{2,1,0:T(2,128)} reshape(f32[2,2,16,128]{3,2,1,0:T(8,128)} %fused.1) | data formatting | bytes 65536 | tf_op jit(solution)/shard_map/reshape | solution.py:544
